TPU v7x, 32 devices: a whole 2x2x4 slice. The times are simulated.
32 devices in a mesh: fsdp: 2 (over y), rows: 8 (over z, core), cols: 2 (over x).
Axes of the slice: x: 2, y: 2, z: 4, core: 2. Of those that a mesh axis runs over, the one named last changes fastest.
Arguments:
- image: bfloat16 [2, 128, 256, 128], P('fsdp', 'rows', 'cols'), may hold values from -6 to 6
- dw_kernel: float32 [7, 7, 128], replicated, may hold values from -0.875 to 0.875
- dw_bias: float32 [128], replicated, may hold values from -3 to 3
- layer_norm_gain: float32 [128], replicated, may hold values from 0.1 to 1.9
- layer_norm_bias: float32 [128], replicated, may hold values from -3 to 3
- w_in: bfloat16 [128, 512], P('fsdp'), may hold values from -0.5 to 0.5
- b_in: float32 [512], replicated, may hold values from -3 to 3
- w_out: bfloat16 [512, 128], P('fsdp'), may hold values from -0.25 to 0.25
- b_out: float32 [128], replicated, may hold values from -3 to 3
- cotangent: bfloat16 [2, 128, 256, 128], P('fsdp', 'rows', 'cols'), may hold values from -60 to 60
Outputs:
- mixed: bfloat16 [2, 128, 256, 128], P('fsdp', 'rows', 'cols')
- d_image: bfloat16 [2, 128, 256, 128], P('fsdp', 'rows', 'cols')
- g_w_in: float32 [128, 512], P('fsdp')
- g_w_out: float32 [512, 128], P('fsdp')
- g_b_in: float32 [512], replicated
- g_kernel: float32 [7, 7, 128], replicated
- g_gain: float32 [128], replicated
All inputs are finite; a program needn't handle non-finite values.
Results may differ from a plain program's by a relative error of at most 0.0057.
Values may be sent and summed in bfloat16 or wider, within the bound.
No kernel may reach another device: no remote copies, remote signals or barrier semaphores. Data moves between devices by JAX's collectives and lax.ppermute only.
A program may use at most 64 MiB of HBM per device.

v0:
```python
import math
import jax
import jax.numpy as jnp
from jax import lax
from jax.sharding import PartitionSpec as P

norm_eps = 1e-06
gelu_coef = math.sqrt(2.0 / math.pi)
cubic_coef = 0.044715


def padded_2(shard, sides, width):
    for axis, dim in sides:
        devices, length = (lax.axis_size(axis), shard.shape[dim])
        up = [(i, (i + 1) % devices) for i in range(devices - 1)]
        down = [(j, i) for i, j in up]
        last = lax.slice_in_dim(shard, length - width, length, axis=dim)
        leading = lax.slice_in_dim(shard, 0, width, axis=dim)
        before = lax.ppermute(last, axis, up)
        after = lax.ppermute(leading, axis, down)
        shard = jnp.concatenate([before, shard, after], axis=dim)
    return shard


def depthwise_taps(padded, kernel, height, width):
    total = jnp.zeros((height, width, padded.shape[2]), jnp.float32)
    for row_tap in range(7):
        for col_tap in range(7):
            total = (
                total
                + padded[row_tap : row_tap + height, col_tap : col_tap + width]
                * kernel[row_tap, col_tap]
            )
    return total


def transposed_taps(padded, kernel, height, width):
    total = jnp.zeros((height, width, padded.shape[2]), jnp.float32)
    for row_tap in range(7):
        for col_tap in range(7):
            total = (
                total
                + padded[6 - row_tap : 6 - row_tap + height, 6 - col_tap : 6 - col_tap + width]
                * kernel[row_tap, col_tap]
            )
    return total


def gelu_parts(pre):
    inner = gelu_coef * (pre + cubic_coef * pre * pre * pre)
    tanh_val = jnp.tanh(inner)
    value = 0.5 * pre * (1.0 + tanh_val)
    slope = 0.5 * (1.0 + tanh_val) + 0.5 * pre * (1.0 - tanh_val * tanh_val) * gelu_coef * (
        1.0 + 3.0 * cubic_coef * pre * pre
    )
    return (value, slope)


def extend_image(field):
    return padded_2(field, (("rows", 0), ("cols", 1)), 3)


def extend_grad(field):
    return padded_2(field, (("rows", 0), ("cols", 1)), 3)


def on_device(
    image, dw_kernel, dw_bias, layer_norm_gain, layer_norm_bias, w_in, b_in, w_out, b_out, cotangent
):
    contract_rows = (((0,), (0,)), ((), ()))
    contract_cols = (((1,), (1,)), ((), ()))
    field = image[0]
    upstream = cotangent[0]
    height, width, channel_count = field.shape
    padded_f = extend_image(field).astype(jnp.float32)
    conv = depthwise_taps(padded_f, dw_kernel, height, width) + dw_bias
    center = jnp.mean(conv, axis=-1, keepdims=True)
    variance_spread = conv - center
    inverse_deviation = lax.rsqrt(
        jnp.mean(variance_spread * variance_spread, axis=-1, keepdims=True) + norm_eps
    )
    standardized_input = variance_spread * inverse_deviation
    normalized_input = (
        (standardized_input * layer_norm_gain + layer_norm_bias)
        .astype(jnp.bfloat16)
        .reshape(-1, channel_count)
    )
    full_in, full_out = (
        lax.all_gather(w_in, "fsdp", axis=0, tiled=True),
        lax.all_gather(w_out, "fsdp", axis=0, tiled=True),
    )
    pre = jnp.dot(normalized_input, full_in, preferred_element_type=jnp.float32) + b_in
    value, slope = gelu_parts(pre)
    hidden = value.astype(jnp.bfloat16)
    mixed = (
        field.reshape(-1, channel_count).astype(jnp.float32)
        + jnp.dot(hidden, full_out, preferred_element_type=jnp.float32)
        + b_out
    )
    mixed = mixed.astype(jnp.bfloat16).reshape(height, width, channel_count)
    flat_up = upstream.reshape(-1, channel_count)
    d_hidden = lax.dot_general(flat_up, full_out, contract_cols, preferred_element_type=jnp.float32)
    d_pre = (d_hidden * slope).astype(jnp.bfloat16)
    normalized_gradient = lax.dot_general(
        d_pre, full_in, contract_cols, preferred_element_type=jnp.float32
    ).reshape(height, width, channel_count)
    gain_product = jnp.sum(normalized_gradient * standardized_input, axis=(0, 1))
    centered_scaled_gradient = normalized_gradient * layer_norm_gain
    convolution_gradient = (
        inverse_deviation
        * (
            centered_scaled_gradient
            - jnp.mean(centered_scaled_gradient, axis=-1, keepdims=True)
            - standardized_input
            * jnp.mean(centered_scaled_gradient * standardized_input, axis=-1, keepdims=True)
        )
    ).astype(jnp.bfloat16)
    bias_term = jnp.sum(d_pre.astype(jnp.float32), axis=0)
    grad_padded = extend_grad(convolution_gradient).astype(jnp.float32)
    d_image = (
        upstream.astype(jnp.float32) + transposed_taps(grad_padded, dw_kernel, height, width)
    ).astype(jnp.bfloat16)
    conv_grad = convolution_gradient.astype(jnp.float32)
    kernel_rows = []
    for row_tap in range(7):
        for col_tap in range(7):
            kernel_rows.append(
                jnp.sum(
                    padded_f[row_tap : row_tap + height, col_tap : col_tap + width] * conv_grad,
                    axis=(0, 1),
                )
            )
    kernel_term = jnp.stack(kernel_rows).reshape(7, 7, channel_count)
    in_rows = w_in.shape[0]
    out_rows = w_out.shape[0]
    term_in = lax.dot_general(
        normalized_input, d_pre, contract_rows, preferred_element_type=jnp.float32
    )
    term_out = lax.dot_general(hidden, flat_up, contract_rows, preferred_element_type=jnp.float32)
    total_in, total_out, g_b_in, g_kernel, g_gain = lax.psum(
        (term_in, term_out, bias_term, kernel_term, gain_product), ("fsdp", "rows", "cols")
    )
    owner = lax.axis_index("fsdp")
    g_w_in = lax.dynamic_slice_in_dim(total_in, owner * in_rows, in_rows, 0)
    g_w_out = lax.dynamic_slice_in_dim(total_out, owner * out_rows, out_rows, 0)
    return (mixed[None], d_image[None], g_w_in, g_w_out, g_b_in, g_kernel, g_gain)


def solution(mesh):
    return jax.shard_map(
        on_device,
        mesh=mesh,
        in_specs=(
            P("fsdp", "rows", "cols", None),
            P(),
            P(),
            P(),
            P(),
            P("fsdp", None),
            P(),
            P("fsdp", None),
            P(),
            P("fsdp", "rows", "cols", None),
        ),
        out_specs=(
            P("fsdp", "rows", "cols", None),
            P("fsdp", "rows", "cols", None),
            P("fsdp", None),
            P("fsdp", None),
            P(),
            P(),
            P(),
        ),
        check_vma=False,
    )
```

profile of v0, /device:TPU:0, one launch (start us, length us, event | category | flops | bytes accessed | tf_op | source)
XLA Modules:
  0.0 208.9 jit_solution(18088232705827283579)
XLA Ops:
  7.2 0.0 all-reduce.4.cloned.1.call-start
  7.2 1.0 slice_bitcast_fusion.1
  8.2 2.4 %collective-permute-start = (bf16[3,128,128]{2,1,0:T(8,128)(2,1)S(1)}, bf16[3,128,128]{2,1,0:T(8,128)(2,1)S(1)}, u32[]{:S(2)}, u32[]{:S(2)}) collective-permute-start(bf16[3,128,128]{2,1,0:T(8,128)(2,1)S(1)} %get-tuple-element.72), channel_id=1, source_target_pairs={{0,2},{2,4},{4,6},{6,8},{8,10},{10,12},{12,14},{1,3},{3,5},{5,7},{... | collective-permute-start | bytes 294920 | tf_op jit(solution)/shard_map/ppermute | solution.py:19
  10.6 1.3 collective-permute-start.1
  11.9 1.0 slice_bitcast_fusion.49
  12.9 1.0 slice_bitcast_fusion.50
  13.9 0.9 slice_bitcast_fusion.48
  14.8 5.5 %all_gather.6 = bf16[128,512]{1,0:T(8,128)(2,1)S(1)} all-gather(bf16[64,512]{1,0:T(8,128)(2,1)} %param.15), channel_id=1, replica_groups=mesh['fsdp'=2,'rows'=8,'cols'=2] {'fsdp'}, dimensions={0}, use_global_device_ids=true | all-gather | bytes 196608 | tf_op jit(solution)/shard_map/all_gather | solution.py:89
  20.3 0.0 collective-permute-done
  20.3 0.0 collective-permute-done.1
  20.3 0.8 pad_maximum_fusion.5
  21.1 3.8 %collective-permute-start.2 = (bf16[22,3,128]{2,1,0:T(4,128)(2,1)S(1)}, bf16[22,3,128]{2,1,0:T(4,128)(2,1)S(1)}, u32[]{:S(2)}, u32[]{:S(2)}) collective-permute-start(bf16[22,3,128]{2,1,0:T(4,128)(2,1)S(1)} %get-tuple-element.68), channel_id=1, source_target_pairs={{0,1},{2,3},{4,5},{6,7},{8,9},{10,11},{12,13},{14,15},{16,17},{18,... | collective-permute-start | bytes 50696 | tf_op jit(solution)/shard_map/ppermute | solution.py:19
  25.0 1.3 collective-permute-start.3
  26.3 5.8 %all_gather.7 = bf16[512,128]{1,0:T(8,128)(2,1)S(1)} all-gather(bf16[256,128]{1,0:T(8,128)(2,1)} %param.17), channel_id=1, replica_groups=mesh['fsdp'=2,'rows'=8,'cols'=2] {'fsdp'}, dimensions={0}, use_global_device_ids=true | all-gather | bytes 196608 | tf_op jit(solution)/shard_map/all_gather | solution.py:90
  32.0 0.0 collective-permute-done.2
  32.0 1.3 maximum_convert_fusion
  33.3 0.0 copy-start.4
  33.3 0.0 copy-start.5
  33.3 0.0 copy-start.7
  33.3 8.2 %fusion.109 = (f32[16,128]{1,0:T(8,128)S(1)}, f32[16,128,128]{2,1,0:T(8,128)S(1)}) fusion(f32[128]{0:T(128)} %param.12, f32[128]{0:T(128)S(1)} %get-tuple-element.121, f32[22,134,128]{2,1,0:T(8,128)S(1)} %maximum_convert_fusion, f32[128]{0:T(128)S(1)} %get-tuple-element.122, f32[128]{0:T(128)S(1)} %get-tuple-element.75, f32[128]{0:T(128)S(1)} %get-tuple-element.76, ...), kind=kLoop, calls=%fused_computation.285 | loop fusion | flops 25950208 | bytes 52462592 | tf_op jit(solution)/shard_map/reduce_sum | solution.py:77
  41.6 0.6 multiply_reduce_fusion.3
  42.2 0.6 add_convert_fusion
  42.9 0.0 copy-start.2
  42.9 1.8 multiply_convert_fusion
  44.7 3.1 %convert_reduce_fusion = (f32[512]{0:T(512)S(1)}, bf16[2048,512]{1,0:T(8,128)(2,1)S(1)}) fusion(f32[2048,512]{1,0:T(8,128)S(1)} %get-tuple-element.124, f32[512]{0:T(512)S(1)} %copy-done.7, bf16[2048,128]{1,0:T(8,128)(2,1)S(1)} %bitcast.186, bf16[512,128]{1,0:T(8,128)(2,1)S(1)} %all_gather.7), kind=kOutput, calls=%fused_computation.58 | convolution fusion | flops 291503616 | bytes 6950912 | tf_op jit(solution)/shard_map/dot_general | solution.py:102
  47.8 0.8 multiply_reduce_fusion.2
  48.6 1.0 multiply_reduce_fusion
  49.7 3.0 %fusion.56 = (f32[128]{0:T(128)S(1)}, f32[128]{0:T(128)S(1)}, f32[128]{0:T(128)S(1)}, f32[128]{0:T(128)S(1)}, f32[128]{0:T(128)S(1)}, /*index=5*/f32[128]{0:T(12...) fusion(f32[22,134,128]{2,1,0:T(8,128)S(1)} %maximum_convert_fus, ...), kind=kLoop, calls=%fused_computation.110 | loop fusion | flops 11794176 | bytes 21538304 | tf_op jit(solution)/shard_map/reduce_sum | solution.py:128
  52.7 2.4 %fusion.57 = (f32[128]{0:T(128)S(1)}, f32[128]{0:T(128)S(1)}, f32[128]{0:T(128)S(1)}, f32[128]{0:T(128)S(1)}, f32[128]{0:T(128)S(1)}, /*index=5*/f32[128]{0:T(12...) fusion(bf16[16,128,128]{2,1,0:T(8,128)(2,1)S(1)} %get-tuple-ele, ...), kind=kLoop, calls=%fused_computation.111 | loop fusion | flops 9697024 | bytes 19407872 | tf_op jit(solution)/shard_map/reduce_sum | solution.py:128
  55.1 1.7 fusion.55
  56.8 0.0 copy-start.1
  56.8 0.0 copy-start.6
  56.8 1.2 fusion.111
  58.0 2.0 collective-permute-start.4
  60.1 1.3 collective-permute-start.5
  61.4 1.5 fusion.112
  62.8 0.0 all-reduce.4.cloned.1.call-update
  62.9 3.4 %collective-permute-done.5 = bf16[3,128,128]{2,1,0:T(8,128)(2,1)S(1)} collective-permute-done((bf16[3,128,128]{2,1,0:T(8,128)(2,1)S(1)}, bf16[3,128,128]{2,1,0:T(8,128)(2,1)S(1)}, u32[]{:S(2)}, u32[]{:S(2)}) %collective-permute-start.5) | collective-permute-done | bytes 98336 | tf_op jit(solution)/shard_map/ppermute | solution.py:20
  66.3 4.5 %collective-permute-start.6 = (bf16[22,3,128]{2,1,0:T(4,128)(2,1)S(1)}, bf16[22,3,128]{2,1,0:T(4,128)(2,1)S(1)}, u32[]{:S(2)}, u32[]{:S(2)}) collective-permute-start(bf16[22,3,128]{2,1,0:T(4,128)(2,1)S(1)} %get-tuple-element.66), channel_id=1, source_target_pairs={{0,1},{2,3},{4,5},{6,7},{8,9},{10,11},{12,13},{14,15},{16,17},{18,... | collective-permute-start | bytes 50696 | tf_op jit(solution)/shard_map/ppermute | solution.py:19
  70.8 1.5 collective-permute-start.7
  72.3 3.1 %fusion.8 = bf16[2048,128]{1,0:T(8,128)(2,1)} fusion(bf16[2048,512]{1,0:T(8,128)(2,1)} %copy-done, bf16[512,128]{1,0:T(8,128)(2,1)S(1)} %all_gather.7, bf16[2048,128]{1,0:T(8,128)(2,1)S(1)} %bitcast.185, f32[128]{0:T(128)S(1)} %copy-done.6), kind=kOutput, calls=%fused_computation.62 | convolution fusion | flops 269484032 | bytes 3277312 | tf_op jit(solution)/shard_map/dot_general | solution.py:97
  75.4 0.1 stack.199
  75.5 43.9 %all-reduce = (f32[512]{0:T(512)}, f32[7,7,128]{2,1,0:T(8,128)}, f32[128]{0:T(128)}) all-reduce(f32[512]{0:T(512)S(1)} %get-tuple-element.127, f32[7,7,128]{2,1,0:T(8,128)S(1)} %reshape.62, f32[128]{0:T(128)S(1)} %get-tuple-element.56), channel_id=1, replica_groups=mesh['fsdp'=2,'rows'=8,'cols'=2] {'fsdp','rows','cols'}, use_global_device_ids=true, to_apply=%region_7.0 | all-reduce | flops 6912 | bytes 55296 | tf_op jit(solution)/shard_map/psum | solution.py:140
  119.5 0.2 maximum_convert_fusion.1
  119.7 8.1 %fusion.108 = bf16[1,16,128,128]{3,2,1,0:T(8,128)(2,1)} fusion(f32[128]{0:T(128)S(1)} %get-tuple-element.121, f32[22,134,128]{2,1,0:T(8,128)S(1)} %maximum_convert_fusion.1, f32[128]{0:T(128)S(1)} %get-tuple-element.122, f32[128]{0:T(128)S(1)} %get-tuple-element.75, f32[128]{0:T(128)S(1)} %get-tuple-element.76, f32[128]{0:T(128)S(1)} %get-tuple-element.77, ...), kind=kLoop, calls=%fused_computation.221 | loop fusion | flops 26214400 | bytes 52453888 | tf_op jit(solution)/shard_map/broadcast_in_dim | solution.py:146
  127.9 71.1 %all-reduce.4.cloned.1.call-done = (f32[128,512]{1,0:T(8,128)}, f32[512,128]{1,0:T(8,128)}) async-done(((f32[128,512]{1,0:T(8,128)}, f32[512,128]{1,0:T(8,128)}), (f32[128,512]{1,0:T(8,128)}, f32[512,128]{1,0:T(8,128)})) %all-reduce.4.cloned.1.call-update) | async-done | bytes 524304 | tf_op jit(solution)/shard_map/psum | solution.py:140
  199.0 1.6 constant_dynamic-slice_fusion
  200.5 1.6 constant_dynamic-slice_fusion.1
  (21 shorter events, 0.1 us)
Async XLA Ops:
  7.2 191.8 %all-reduce.4.cloned.1.call-start = ((), (), s32[]{:S(2)}) async-start(), calls=%async_computation | async-start | bytes 1048576 | tf_op jit(solution)/shard_map/psum | solution.py:140
  8.2 12.1 %collective-permute-start = (bf16[3,128,128]{2,1,0:T(8,128)(2,1)S(1)}, bf16[3,128,128]{2,1,0:T(8,128)(2,1)S(1)}, u32[]{:S(2)}, u32[]{:S(2)}) collective-permute-start(bf16[3,128,128]{2,1,0:T(8,128)(2,1)S(1)} %get-tuple-element.72), channel_id=1, source_target_pairs={{0,2},{2,4},{4,6},{6,8},{8,10},{10,12},{12,14},{1,3},{3,5},{5,7},{... | collective-permute-start | bytes 294920 | tf_op jit(solution)/shard_map/ppermute | solution.py:19
  10.6 9.7 %collective-permute-start.1 = (bf16[3,128,128]{2,1,0:T(8,128)(2,1)S(1)}, bf16[3,128,128]{2,1,0:T(8,128)(2,1)S(1)}, u32[]{:S(2)}, u32[]{:S(2)}) collective-permute-start(bf16[3,128,128]{2,1,0:T(8,128)(2,1)S(1)} %get-tuple-element.73), channel_id=1, source_target_pairs={{2,0},{4,2},{6,4},{8,6},{10,8},{12,10},{14,12},{3,1},{5,3},{7,5},{... | collective-permute-start | bytes 294920 | tf_op jit(solution)/shard_map/ppermute | solution.py:20
  21.1 10.9 %collective-permute-start.2 = (bf16[22,3,128]{2,1,0:T(4,128)(2,1)S(1)}, bf16[22,3,128]{2,1,0:T(4,128)(2,1)S(1)}, u32[]{:S(2)}, u32[]{:S(2)}) collective-permute-start(bf16[22,3,128]{2,1,0:T(4,128)(2,1)S(1)} %get-tuple-element.68), channel_id=1, source_target_pairs={{0,1},{2,3},{4,5},{6,7},{8,9},{10,11},{12,13},{14,15},{16,17},{18,... | collective-permute-start | bytes 50696 | tf_op jit(solution)/shard_map/ppermute | solution.py:19
  25.0 7.1 %collective-permute-start.3 = (bf16[22,3,128]{2,1,0:T(4,128)(2,1)S(1)}, bf16[22,3,128]{2,1,0:T(4,128)(2,1)S(1)}, u32[]{:S(2)}, u32[]{:S(2)}) collective-permute-start(bf16[22,3,128]{2,1,0:T(4,128)(2,1)S(1)} %get-tuple-element.69), channel_id=1, source_target_pairs={{1,0},{3,2},{5,4},{7,6},{9,8},{11,10},{13,12},{15,14},{17,16},{19,... | collective-permute-start | bytes 50696 | tf_op jit(solution)/shard_map/ppermute | solution.py:20
  33.3 8.9 %copy-start.4 = (f32[128]{0:T(128)S(1)}, f32[128]{0:T(128)}, u32[]{:S(2)}) copy-start(f32[128]{0:T(128)} %param.13) | copy-start | bytes 1540
  33.3 8.9 %copy-start.5 = (f32[128]{0:T(128)S(1)}, f32[128]{0:T(128)}, u32[]{:S(2)}) copy-start(f32[128]{0:T(128)} %param.14) | copy-start | bytes 1540
  33.3 9.5 %copy-start.7 = (f32[512]{0:T(512)S(1)}, f32[512]{0:T(512)}, u32[]{:S(2)}) copy-start(f32[512]{0:T(512)} %param.16) | copy-start | bytes 6148
  42.9 1.8 copy-start.2
  44.7 16.7 %copy-start = (bf16[2048,512]{1,0:T(8,128)(2,1)}, bf16[2048,512]{1,0:T(8,128)(2,1)S(1)}, u32[]{:S(2)}) copy-start(bf16[2048,512]{1,0:T(8,128)(2,1)S(1)} %get-tuple-element.123) | copy-start | bytes 6291460
  56.8 15.5 %copy-start.1 = (bf16[1,16,128,128]{3,2,1,0:T(8,128)(2,1)S(1)}, bf16[1,16,128,128]{3,2,1,0:T(8,128)(2,1)}, u32[]{:S(2)}) copy-start(bf16[1,16,128,128]{3,2,1,0:T(8,128)(2,1)} %param.10) | copy-start | bytes 1572868
  56.8 15.5 %copy-start.6 = (f32[128]{0:T(128)S(1)}, f32[128]{0:T(128)}, u32[]{:S(2)}) copy-start(f32[128]{0:T(128)} %param.18) | copy-start | bytes 1540
  58.0 4.8 %collective-permute-start.4 = (bf16[3,128,128]{2,1,0:T(8,128)(2,1)S(1)}, bf16[3,128,128]{2,1,0:T(8,128)(2,1)S(1)}, u32[]{:S(2)}, u32[]{:S(2)}) collective-permute-start(bf16[3,128,128]{2,1,0:T(8,128)(2,1)S(1)} %get-tuple-element.70), channel_id=1, source_target_pairs={{0,2},{2,4},{4,6},{6,8},{8,10},{10,12},{12,14},{1,3},{3,5},{5,7},{... | collective-permute-start | bytes 294920 | tf_op jit(solution)/shard_map/ppermute | solution.py:19
  60.1 6.2 %collective-permute-start.5 = (bf16[3,128,128]{2,1,0:T(8,128)(2,1)S(1)}, bf16[3,128,128]{2,1,0:T(8,128)(2,1)S(1)}, u32[]{:S(2)}, u32[]{:S(2)}) collective-permute-start(bf16[3,128,128]{2,1,0:T(8,128)(2,1)S(1)} %get-tuple-element.71), channel_id=1, source_target_pairs={{2,0},{4,2},{6,4},{8,6},{10,8},{12,10},{14,12},{3,1},{5,3},{7,5},{... | collective-permute-start | bytes 294920 | tf_op jit(solution)/shard_map/ppermute | solution.py:20
  62.8 56.9 %copy-start.3 = (bf16[1,16,128,128]{3,2,1,0:T(8,128)(2,1)S(1)}, bf16[1,16,128,128]{3,2,1,0:T(8,128)(2,1)}, u32[]{:S(2)}) copy-start(bf16[1,16,128,128]{3,2,1,0:T(8,128)(2,1)} %param.19) | copy-start | bytes 1572868
  66.3 53.2 %collective-permute-start.6 = (bf16[22,3,128]{2,1,0:T(4,128)(2,1)S(1)}, bf16[22,3,128]{2,1,0:T(4,128)(2,1)S(1)}, u32[]{:S(2)}, u32[]{:S(2)}) collective-permute-start(bf16[22,3,128]{2,1,0:T(4,128)(2,1)S(1)} %get-tuple-element.66), channel_id=1, source_target_pairs={{0,1},{2,3},{4,5},{6,7},{8,9},{10,11},{12,13},{14,15},{16,17},{18,... | collective-permute-start | bytes 50696 | tf_op jit(solution)/shard_map/ppermute | solution.py:19
  70.8 48.7 %collective-permute-start.7 = (bf16[22,3,128]{2,1,0:T(4,128)(2,1)S(1)}, bf16[22,3,128]{2,1,0:T(4,128)(2,1)S(1)}, u32[]{:S(2)}, u32[]{:S(2)}) collective-permute-start(bf16[22,3,128]{2,1,0:T(4,128)(2,1)S(1)} %get-tuple-element.67), channel_id=1, source_target_pairs={{1,0},{3,2},{5,4},{7,6},{9,8},{11,10},{13,12},{15,14},{17,16},{19,... | collective-permute-start | bytes 50696 | tf_op jit(solution)/shard_map/ppermute | solution.py:20
Sparse Core Ops, SparseCore 0:
  63.0 135.9 all-reduce.3
where the time goes:
time: 210 us; the launch traced here: 209 us
  waiting for transfers between devices  74.5 us (35%)
  blocking collectives  55.2 us (26%)
  other arithmetic  28 us (13%)
  starting transfers between devices  18.2 us (9%)
  between operations  14.4 us (7%)
  matrix products  11.5 us (5%)
  local copies, waits for them, and re-layouts  7.18 us (3%)
    psum x1, waiting for transfers between devices, on_device(): lax.psum((term_in, term_out, bias_term, kernel_term, gain_product), ('fsd...  71.1 us
    psum x1, blocking collectives, on_device(): lax.psum((term_in, term_out, bias_term, kernel_term, gain_product), ('fsd...  43.9 us
    ppermute x4, starting transfers between devices, padded_2(): before = lax.ppermute(last, axis, up)  12.8 us
    reduce_sum x1, other arithmetic, on_device(): center = jnp.mean(conv, axis=-1, keepdims=True)  8.22 us
    broadcast_in_dim x1, other arithmetic, on_device(): d_image[None]  8.14 us
    reduce_sum x3, other arithmetic, on_device(): jnp.sum(padded_f[row_tap:row_tap + height, col_tap:col_tap + width] * con...  7.12 us
    all_gather x1, blocking collectives, on_device(): lax.all_gather(w_out, 'fsdp', axis=0, tiled=True)  5.77 us
    all_gather x1, blocking collectives, on_device(): lax.all_gather(w_in, 'fsdp', axis=0, tiled=True)  5.51 us
  transfers between devices with their start and end apart: 9, of which 2 were waited for; matrix products, arithmetic and copies ran while one was open for 8% of the time, Pallas kernels for 0%

commit v1 on v0

--- a/solution.py
+++ b/solution.py
@@ -138,7 +138,8 @@
     )
     term_out = lax.dot_general(hidden, flat_up, contract_rows, preferred_element_type=jnp.float32)
     total_in, total_out, g_b_in, g_kernel, g_gain = lax.psum(
-        (term_in, term_out, bias_term, kernel_term, gain_product), ("fsdp", "rows", "cols")
+        lax.psum((term_in, term_out, bias_term, kernel_term, gain_product), ("rows", "cols")),
+        "fsdp",
     )
     owner = lax.axis_index("fsdp")
     g_w_in = lax.dynamic_slice_in_dim(total_in, owner * in_rows, in_rows, 0)

time: 210 us -> 202 us (0.962)
  waiting for transfers between devices: 74.5 us -> 40.2 us
  blocking collectives: 55.2 us -> 82.3 us
    psum x1 -> x2, waiting for transfers between devices: 71.1 us -> 36.8 us  [the longest x1 23.4 us: on_device(): lax.psum(lax.psum((term_in, term_out, bias_term, kernel_term, gain_produc...]
    psum x1 -> x2, blocking collectives: 43.9 us -> 71 us  [the longest x1 62.1 us: on_device(): lax.psum((term_in, term_out, bias_term, kernel_term, gain_product), ('row...]
  transfers between devices with their start and end apart: 9 -> 10, of which waited for: 2 -> 3; matrix products, arithmetic and copies ran while one was open for 8% -> 8% of each run, Pallas kernels for 0% -> 0%
where the time goes in v1:
time: 202 us
  blocking collectives  82.3 us (41%)
  waiting for transfers between devices  40.2 us (20%)
  other arithmetic  28 us (14%)
  starting transfers between devices  18.2 us (9%)
  between operations  14.4 us (7%)
  matrix products  11.4 us (6%)
  local copies, waits for them, and re-layouts  7.18 us (4%)
    psum x1, blocking collectives, on_device(): lax.psum((term_in, term_out, bias_term, kernel_term, gain_product), ('row...  62.1 us
    psum x1, waiting for transfers between devices, on_device(): lax.psum(lax.psum((term_in, term_out, bias_term, kernel_term, gain_produc...  23.4 us
    psum x1, waiting for transfers between devices, on_device(): lax.psum((term_in, term_out, bias_term, kernel_term, gain_product), ('row...  13.4 us
    ppermute x4, starting transfers between devices, padded_2(): before = lax.ppermute(last, axis, up)  13 us
    psum x1, blocking collectives, on_device(): lax.psum(lax.psum((term_in, term_out, bias_term, kernel_term, gain_produc...  8.96 us
    reduce_sum x1, other arithmetic, on_device(): center = jnp.mean(conv, axis=-1, keepdims=True)  8.22 us
    broadcast_in_dim x1, other arithmetic, on_device(): d_image[None]  8.14 us
    reduce_sum x3, other arithmetic, on_device(): jnp.sum(padded_f[row_tap:row_tap + height, col_tap:col_tap + width] * con...  7.12 us
  transfers between devices with their start and end apart: 10, of which 3 were waited for; matrix products, arithmetic and copies ran while one was open for 8% of the time, Pallas kernels for 0%

profile of v1, /device:TPU:0, one launch (start us, length us, event | category | flops | bytes accessed | tf_op | source)
XLA Modules:
  0.0 201.8 jit_solution(14206072131309521005)
XLA Ops:
  7.2 0.0 all-reduce.7.cloned.1.call-start
  7.2 1.0 slice_bitcast_fusion.1
  8.2 2.4 %collective-permute-start = (bf16[3,128,128]{2,1,0:T(8,128)(2,1)S(1)}, bf16[3,128,128]{2,1,0:T(8,128)(2,1)S(1)}, u32[]{:S(2)}, u32[]{:S(2)}) collective-permute-start(bf16[3,128,128]{2,1,0:T(8,128)(2,1)S(1)} %get-tuple-element.77), channel_id=1, source_target_pairs={{0,2},{2,4},{4,6},{6,8},{8,10},{10,12},{12,14},{1,3},{3,5},{5,7},{... | collective-permute-start | bytes 294920 | tf_op jit(solution)/shard_map/ppermute | solution.py:19
  10.6 1.3 collective-permute-start.1
  11.9 1.0 slice_bitcast_fusion.49
  12.9 1.0 slice_bitcast_fusion.50
  13.9 0.9 slice_bitcast_fusion.48
  14.8 5.5 %all_gather.6 = bf16[128,512]{1,0:T(8,128)(2,1)S(1)} all-gather(bf16[64,512]{1,0:T(8,128)(2,1)} %param.15), channel_id=1, replica_groups=mesh['fsdp'=2,'rows'=8,'cols'=2] {'fsdp'}, dimensions={0}, use_global_device_ids=true | all-gather | bytes 196608 | tf_op jit(solution)/shard_map/all_gather | solution.py:89
  20.3 0.8 pad_maximum_fusion.5
  21.1 3.8 %collective-permute-start.2 = (bf16[22,3,128]{2,1,0:T(4,128)(2,1)S(1)}, bf16[22,3,128]{2,1,0:T(4,128)(2,1)S(1)}, u32[]{:S(2)}, u32[]{:S(2)}) collective-permute-start(bf16[22,3,128]{2,1,0:T(4,128)(2,1)S(1)} %get-tuple-element.73), channel_id=1, source_target_pairs={{0,1},{2,3},{4,5},{6,7},{8,9},{10,11},{12,13},{14,15},{16,17},{18,... | collective-permute-start | bytes 50696 | tf_op jit(solution)/shard_map/ppermute | solution.py:19
  25.0 1.3 collective-permute-start.3
  26.3 5.8 %all_gather.7 = bf16[512,128]{1,0:T(8,128)(2,1)S(1)} all-gather(bf16[256,128]{1,0:T(8,128)(2,1)} %param.17), channel_id=1, replica_groups=mesh['fsdp'=2,'rows'=8,'cols'=2] {'fsdp'}, dimensions={0}, use_global_device_ids=true | all-gather | bytes 196608 | tf_op jit(solution)/shard_map/all_gather | solution.py:90
  32.0 1.3 maximum_convert_fusion
  33.3 0.0 copy-start.4
  33.3 0.0 copy-start.5
  33.3 0.0 copy-start.7
  33.3 8.2 %fusion.109 = (f32[16,128]{1,0:T(8,128)S(1)}, f32[16,128,128]{2,1,0:T(8,128)S(1)}) fusion(f32[128]{0:T(128)} %param.12, f32[128]{0:T(128)S(1)} %get-tuple-element.126, f32[22,134,128]{2,1,0:T(8,128)S(1)} %maximum_convert_fusion, f32[128]{0:T(128)S(1)} %get-tuple-element.127, f32[128]{0:T(128)S(1)} %get-tuple-element.80, f32[128]{0:T(128)S(1)} %get-tuple-element.81, ...), kind=kLoop, calls=%fused_computation.285 | loop fusion | flops 25950208 | bytes 52462592 | tf_op jit(solution)/shard_map/reduce_sum | solution.py:77
  41.6 0.6 multiply_reduce_fusion.3
  42.2 0.6 add_convert_fusion
  42.9 0.0 copy-start.2
  42.9 1.8 multiply_convert_fusion
  44.7 3.1 %convert_reduce_fusion = (f32[512]{0:T(512)S(1)}, bf16[2048,512]{1,0:T(8,128)(2,1)S(1)}) fusion(f32[2048,512]{1,0:T(8,128)S(1)} %get-tuple-element.129, f32[512]{0:T(512)S(1)} %copy-done.7, bf16[2048,128]{1,0:T(8,128)(2,1)S(1)} %bitcast.186, bf16[512,128]{1,0:T(8,128)(2,1)S(1)} %all_gather.7), kind=kOutput, calls=%fused_computation.58 | convolution fusion | flops 291503616 | bytes 6950912 | tf_op jit(solution)/shard_map/dot_general | solution.py:102
  47.8 0.8 multiply_reduce_fusion.2
  48.6 1.0 multiply_reduce_fusion
  49.7 3.0 %fusion.56 = (f32[128]{0:T(128)S(1)}, f32[128]{0:T(128)S(1)}, f32[128]{0:T(128)S(1)}, f32[128]{0:T(128)S(1)}, f32[128]{0:T(128)S(1)}, /*index=5*/f32[128]{0:T(12...) fusion(f32[22,134,128]{2,1,0:T(8,128)S(1)} %maximum_convert_fus, ...), kind=kLoop, calls=%fused_computation.110 | loop fusion | flops 11794176 | bytes 21538304 | tf_op jit(solution)/shard_map/reduce_sum | solution.py:128
  52.7 2.4 %fusion.57 = (f32[128]{0:T(128)S(1)}, f32[128]{0:T(128)S(1)}, f32[128]{0:T(128)S(1)}, f32[128]{0:T(128)S(1)}, f32[128]{0:T(128)S(1)}, /*index=5*/f32[128]{0:T(12...) fusion(bf16[16,128,128]{2,1,0:T(8,128)(2,1)S(1)} %get-tuple-ele, ...), kind=kLoop, calls=%fused_computation.111 | loop fusion | flops 9697024 | bytes 19407872 | tf_op jit(solution)/shard_map/reduce_sum | solution.py:128
  55.1 1.7 fusion.55
  56.8 0.0 copy-start.6
  56.8 1.2 fusion.111
  58.0 2.0 %collective-permute-start.4 = (bf16[3,128,128]{2,1,0:T(8,128)(2,1)S(1)}, bf16[3,128,128]{2,1,0:T(8,128)(2,1)S(1)}, u32[]{:S(2)}, u32[]{:S(2)}) collective-permute-start(bf16[3,128,128]{2,1,0:T(8,128)(2,1)S(1)} %get-tuple-element.75), channel_id=1, source_target_pairs={{0,2},{2,4},{4,6},{6,8},{8,10},{10,12},{12,14},{1,3},{3,5},{5,7},{... | collective-permute-start | bytes 294920 | tf_op jit(solution)/shard_map/ppermute | solution.py:19
  60.1 1.3 collective-permute-start.5
  61.4 1.5 fusion.112
  62.8 0.0 all-reduce.7.cloned.1.call-update
  62.9 0.0 all-reduce.9.cloned.1.call-start
  62.9 3.3 %collective-permute-done.5 = bf16[3,128,128]{2,1,0:T(8,128)(2,1)S(1)} collective-permute-done((bf16[3,128,128]{2,1,0:T(8,128)(2,1)S(1)}, bf16[3,128,128]{2,1,0:T(8,128)(2,1)S(1)}, u32[]{:S(2)}, u32[]{:S(2)}) %collective-permute-start.5) | collective-permute-done | bytes 98336 | tf_op jit(solution)/shard_map/ppermute | solution.py:20
  66.3 4.7 %collective-permute-start.6 = (bf16[22,3,128]{2,1,0:T(4,128)(2,1)S(1)}, bf16[22,3,128]{2,1,0:T(4,128)(2,1)S(1)}, u32[]{:S(2)}, u32[]{:S(2)}) collective-permute-start(bf16[22,3,128]{2,1,0:T(4,128)(2,1)S(1)} %get-tuple-element.71), channel_id=1, source_target_pairs={{0,1},{2,3},{4,5},{6,7},{8,9},{10,11},{12,13},{14,15},{16,17},{18,... | collective-permute-start | bytes 50696 | tf_op jit(solution)/shard_map/ppermute | solution.py:19
  71.0 1.3 collective-permute-start.7
  72.3 3.1 %fusion.8 = bf16[2048,128]{1,0:T(8,128)(2,1)} fusion(bf16[2048,512]{1,0:T(8,128)(2,1)} %copy-done, bf16[512,128]{1,0:T(8,128)(2,1)S(1)} %all_gather.7, bf16[2048,128]{1,0:T(8,128)(2,1)S(1)} %bitcast.185, f32[128]{0:T(128)S(1)} %copy-done.6), kind=kOutput, calls=%fused_computation.62 | convolution fusion | flops 269484032 | bytes 3277312 | tf_op jit(solution)/shard_map/dot_general | solution.py:97
  75.4 0.1 stack.199
  75.5 62.1 %all-reduce = (f32[512]{0:T(512)S(1)}, f32[7,7,128]{2,1,0:T(8,128)S(1)}, f32[128]{0:T(128)S(1)}) all-reduce(f32[512]{0:T(512)S(1)} %get-tuple-element.132, f32[7,7,128]{2,1,0:T(8,128)S(1)} %reshape.62, f32[128]{0:T(128)S(1)} %get-tuple-element.56), channel_id=1, replica_groups=mesh['fsdp'=2,'rows'=8,'cols'=2] {'rows','cols'}, use_global_device_ids=true, to_apply=%region_9.0 | all-reduce | flops 6912 | bytes 55296 | tf_op jit(solution)/shard_map/psum | solution.py:141
  137.6 9.0 %all-reduce.2 = (f32[512]{0:T(512)}, f32[7,7,128]{2,1,0:T(8,128)}, f32[128]{0:T(128)}) all-reduce(f32[512]{0:T(512)S(1)} %get-tuple-element.58, f32[7,7,128]{2,1,0:T(8,128)S(1)} %get-tuple-element.59, f32[128]{0:T(128)S(1)} %get-tuple-element.60), channel_id=1, replica_groups=mesh['fsdp'=2,'rows'=8,'cols'=2] {'fsdp'}, use_global_device_ids=true, to_apply=%region_10.0 | all-reduce | flops 6912 | bytes 55296 | tf_op jit(solution)/shard_map/psum | solution.py:140
  146.6 0.2 maximum_convert_fusion.1
  146.8 13.4 %all-reduce.7.cloned.1.call-done = (f32[128,512]{1,0:T(8,128)}, f32[512,128]{1,0:T(8,128)}) async-done(((f32[128,512]{1,0:T(8,128)}, f32[512,128]{1,0:T(8,128)}), (f32[128,512]{1,0:T(8,128)}, f32[512,128]{1,0:T(8,128)})) %all-reduce.7.cloned.1.call-update) | async-done | bytes 524304 | tf_op jit(solution)/shard_map/psum | solution.py:141
  160.3 0.0 all-reduce.9.cloned.1.call-update
  160.3 8.1 %fusion.108 = bf16[1,16,128,128]{3,2,1,0:T(8,128)(2,1)} fusion(f32[128]{0:T(128)S(1)} %get-tuple-element.126, f32[22,134,128]{2,1,0:T(8,128)S(1)} %maximum_convert_fusion.1, f32[128]{0:T(128)S(1)} %get-tuple-element.127, f32[128]{0:T(128)S(1)} %get-tuple-element.80, f32[128]{0:T(128)S(1)} %get-tuple-element.81, f32[128]{0:T(128)S(1)} %get-tuple-element.82, ...), kind=kLoop, calls=%fused_computation.221 | loop fusion | flops 26214400 | bytes 52453888 | tf_op jit(solution)/shard_map/broadcast_in_dim | solution.py:147
  168.4 23.4 %all-reduce.9.cloned.1.call-done = (f32[128,512]{1,0:T(8,128)}, f32[512,128]{1,0:T(8,128)}) async-done(((f32[128,512]{1,0:T(8,128)}, f32[512,128]{1,0:T(8,128)}), (f32[128,512]{1,0:T(8,128)}, f32[512,128]{1,0:T(8,128)})) %all-reduce.9.cloned.1.call-update) | async-done | bytes 524304 | tf_op jit(solution)/shard_map/psum | solution.py:140
  191.8 1.6 constant_dynamic-slice_fusion
  193.4 1.6 constant_dynamic-slice_fusion.1
  (25 shorter events, 0.1 us)
Async XLA Ops:
  7.2 153.1 %all-reduce.7.cloned.1.call-start = ((), (), s32[]{:S(2)}) async-start(), calls=%async_computation | async-start | bytes 1048576 | tf_op jit(solution)/shard_map/psum | solution.py:141
  8.2 12.1 %collective-permute-start = (bf16[3,128,128]{2,1,0:T(8,128)(2,1)S(1)}, bf16[3,128,128]{2,1,0:T(8,128)(2,1)S(1)}, u32[]{:S(2)}, u32[]{:S(2)}) collective-permute-start(bf16[3,128,128]{2,1,0:T(8,128)(2,1)S(1)} %get-tuple-element.77), channel_id=1, source_target_pairs={{0,2},{2,4},{4,6},{6,8},{8,10},{10,12},{12,14},{1,3},{3,5},{5,7},{... | collective-permute-start | bytes 294920 | tf_op jit(solution)/shard_map/ppermute | solution.py:19
  10.6 9.7 %collective-permute-start.1 = (bf16[3,128,128]{2,1,0:T(8,128)(2,1)S(1)}, bf16[3,128,128]{2,1,0:T(8,128)(2,1)S(1)}, u32[]{:S(2)}, u32[]{:S(2)}) collective-permute-start(bf16[3,128,128]{2,1,0:T(8,128)(2,1)S(1)} %get-tuple-element.78), channel_id=1, source_target_pairs={{2,0},{4,2},{6,4},{8,6},{10,8},{12,10},{14,12},{3,1},{5,3},{7,5},{... | collective-permute-start | bytes 294920 | tf_op jit(solution)/shard_map/ppermute | solution.py:20
  21.1 10.9 %collective-permute-start.2 = (bf16[22,3,128]{2,1,0:T(4,128)(2,1)S(1)}, bf16[22,3,128]{2,1,0:T(4,128)(2,1)S(1)}, u32[]{:S(2)}, u32[]{:S(2)}) collective-permute-start(bf16[22,3,128]{2,1,0:T(4,128)(2,1)S(1)} %get-tuple-element.73), channel_id=1, source_target_pairs={{0,1},{2,3},{4,5},{6,7},{8,9},{10,11},{12,13},{14,15},{16,17},{18,... | collective-permute-start | bytes 50696 | tf_op jit(solution)/shard_map/ppermute | solution.py:19
  25.0 7.1 %collective-permute-start.3 = (bf16[22,3,128]{2,1,0:T(4,128)(2,1)S(1)}, bf16[22,3,128]{2,1,0:T(4,128)(2,1)S(1)}, u32[]{:S(2)}, u32[]{:S(2)}) collective-permute-start(bf16[22,3,128]{2,1,0:T(4,128)(2,1)S(1)} %get-tuple-element.74), channel_id=1, source_target_pairs={{1,0},{3,2},{5,4},{7,6},{9,8},{11,10},{13,12},{15,14},{17,16},{19,... | collective-permute-start | bytes 50696 | tf_op jit(solution)/shard_map/ppermute | solution.py:20
  33.3 8.9 %copy-start.4 = (f32[128]{0:T(128)S(1)}, f32[128]{0:T(128)}, u32[]{:S(2)}) copy-start(f32[128]{0:T(128)} %param.13) | copy-start | bytes 1540
  33.3 8.9 %copy-start.5 = (f32[128]{0:T(128)S(1)}, f32[128]{0:T(128)}, u32[]{:S(2)}) copy-start(f32[128]{0:T(128)} %param.14) | copy-start | bytes 1540
  33.3 9.5 %copy-start.7 = (f32[512]{0:T(512)S(1)}, f32[512]{0:T(512)}, u32[]{:S(2)}) copy-start(f32[512]{0:T(512)} %param.16) | copy-start | bytes 6148
  42.9 1.8 copy-start.2
  44.7 16.7 %copy-start = (bf16[2048,512]{1,0:T(8,128)(2,1)}, bf16[2048,512]{1,0:T(8,128)(2,1)S(1)}, u32[]{:S(2)}) copy-start(bf16[2048,512]{1,0:T(8,128)(2,1)S(1)} %get-tuple-element.128) | copy-start | bytes 6291460
  56.8 15.5 %copy-start.1 = (bf16[1,16,128,128]{3,2,1,0:T(8,128)(2,1)S(1)}, bf16[1,16,128,128]{3,2,1,0:T(8,128)(2,1)}, u32[]{:S(2)}) copy-start(bf16[1,16,128,128]{3,2,1,0:T(8,128)(2,1)} %param.10) | copy-start | bytes 1572868
  56.8 15.5 %copy-start.6 = (f32[128]{0:T(128)S(1)}, f32[128]{0:T(128)}, u32[]{:S(2)}) copy-start(f32[128]{0:T(128)} %param.18) | copy-start | bytes 1540
  58.0 4.9 %collective-permute-start.4 = (bf16[3,128,128]{2,1,0:T(8,128)(2,1)S(1)}, bf16[3,128,128]{2,1,0:T(8,128)(2,1)S(1)}, u32[]{:S(2)}, u32[]{:S(2)}) collective-permute-start(bf16[3,128,128]{2,1,0:T(8,128)(2,1)S(1)} %get-tuple-element.75), channel_id=1, source_target_pairs={{0,2},{2,4},{4,6},{6,8},{8,10},{10,12},{12,14},{1,3},{3,5},{5,7},{... | collective-permute-start | bytes 294920 | tf_op jit(solution)/shard_map/ppermute | solution.py:19
  60.1 6.2 %collective-permute-start.5 = (bf16[3,128,128]{2,1,0:T(8,128)(2,1)S(1)}, bf16[3,128,128]{2,1,0:T(8,128)(2,1)S(1)}, u32[]{:S(2)}, u32[]{:S(2)}) collective-permute-start(bf16[3,128,128]{2,1,0:T(8,128)(2,1)S(1)} %get-tuple-element.76), channel_id=1, source_target_pairs={{2,0},{4,2},{6,4},{8,6},{10,8},{12,10},{14,12},{3,1},{5,3},{7,5},{... | collective-permute-start | bytes 294920 | tf_op jit(solution)/shard_map/ppermute | solution.py:20
  62.8 97.5 %copy-start.3 = (bf16[1,16,128,128]{3,2,1,0:T(8,128)(2,1)S(1)}, bf16[1,16,128,128]{3,2,1,0:T(8,128)(2,1)}, u32[]{:S(2)}) copy-start(bf16[1,16,128,128]{3,2,1,0:T(8,128)(2,1)} %param.19) | copy-start | bytes 1572868
  62.9 129.0 %all-reduce.9.cloned.1.call-start = ((), (), s32[]{:S(2)}) async-start(), calls=%async_computation.1 | async-start | bytes 1048576 | tf_op jit(solution)/shard_map/psum | solution.py:140
  66.3 80.3 %collective-permute-start.6 = (bf16[22,3,128]{2,1,0:T(4,128)(2,1)S(1)}, bf16[22,3,128]{2,1,0:T(4,128)(2,1)S(1)}, u32[]{:S(2)}, u32[]{:S(2)}) collective-permute-start(bf16[22,3,128]{2,1,0:T(4,128)(2,1)S(1)} %get-tuple-element.71), channel_id=1, source_target_pairs={{0,1},{2,3},{4,5},{6,7},{8,9},{10,11},{12,13},{14,15},{16,17},{18,... | collective-permute-start | bytes 50696 | tf_op jit(solution)/shard_map/ppermute | solution.py:19
  71.0 75.6 %collective-permute-start.7 = (bf16[22,3,128]{2,1,0:T(4,128)(2,1)S(1)}, bf16[22,3,128]{2,1,0:T(4,128)(2,1)S(1)}, u32[]{:S(2)}, u32[]{:S(2)}) collective-permute-start(bf16[22,3,128]{2,1,0:T(4,128)(2,1)S(1)} %get-tuple-element.72), channel_id=1, source_target_pairs={{1,0},{3,2},{5,4},{7,6},{9,8},{11,10},{13,12},{15,14},{17,16},{19,... | collective-permute-start | bytes 50696 | tf_op jit(solution)/shard_map/ppermute | solution.py:20
Sparse Core Ops, SparseCore 0:
  63.0 97.2 all-reduce.6
  162.6 29.1 all-reduce.8
